TPU v7x, 32 devices: a whole 2x2x4 slice. The times are simulated.
32 devices in a mesh: src: 4 (over y, x), snk: 4 (over z), slab: 2 (over core).
Axes of the slice: x: 2, y: 2, z: 4, core: 2. Of those that a mesh axis runs over, the one named last changes fastest.
Arguments:
- eigvecs: bfloat16 [8, 8192, 384], P('snk', ('src', 'slab')), may hold values from -0.125 to 0.125
- perambulator: bfloat16 [8, 8, 4, 192, 384], P('snk', 'src'), may hold values from -0.4375 to 0.4375
- momenta: int32 [4, 3], replicated, may hold values from 1 to 3
- source_times: int32 [8], P('src'), may hold values from 0 to 7, as said below
Outputs:
- blocks: float32 [4, 8, 8, 4, 192, 384], P(None, 'snk', 'src', None, 'slab')
Inputs may be any that keep to these rules, and one draw needn't show every extreme that they name: `source_times`: distinct time slices.
All inputs are finite; a program needn't handle non-finite values.
Results may differ from a plain program's by a relative error of at most 0.0062.
Values may be sent and summed in bfloat16 or wider, within the bound.
No kernel may reach another device: no remote copies, remote signals or barrier semaphores. Data moves between devices by JAX's collectives and lax.ppermute only.
A program may use at most 128 MiB of HBM per device.

v0:
```python
import functools
import math

import jax
import jax.numpy as jnp
from jax import lax
from jax.experimental import pallas as pl
from jax.experimental.pallas import tpu as pltpu
from jax.sharding import PartitionSpec as P


LX = 32
LY = 32
TAIL = 16
CHUNK = 256
F32 = jnp.float32
BF16 = jnp.bfloat16
VMEM = pl.BlockSpec(memory_space=pltpu.VMEM)
SMEM = pl.BlockSpec(memory_space=pltpu.SMEM)


def angles(momenta, xs, ys, zs, lz):
    fx = (momenta[:, 0:1] * xs[None, :] % LX).astype(F32) / LX
    fy = (momenta[:, 1:2] * ys[None, :] % LY).astype(F32) / LY
    fz = (momenta[:, 2:3] * zs[None, :] % lz).astype(F32) / lz
    return 2.0 * math.pi * (fx + fy + fz)


def general(eigvecs, perambulator, momenta, source_times):
    nev = eigvecs.shape[2] // 2
    count = eigvecs.shape[1]
    zpl = count // (LX * LY)
    slabs = lax.axis_size("slab")
    lz = zpl * lax.axis_size("src") * slabs
    sites = jnp.arange(count, dtype=jnp.int32)
    xs = sites % LX
    ys = sites // LX % LY
    zs = sites // (LX * LY) + lax.axis_index(("src", "slab")) * zpl
    angle = angles(momenta, xs, ys, zs, lz)
    vreal = eigvecs[:, :, :nev].astype(F32)
    vimag = eigvecs[:, :, nev:].astype(F32)
    partials = []
    for m in range(angle.shape[0]):
        cosine = jnp.cos(angle[m])[None, :, None]
        sine = jnp.sin(angle[m])[None, :, None]
        phased = jnp.concatenate(
            [cosine * vreal + sine * vimag, cosine * vimag - sine * vreal], axis=2
        ).astype(BF16)
        gram = jnp.einsum("tsa,tsb->tab", eigvecs, phased, preferred_element_type=F32)
        real = gram[:, :nev, :nev] + gram[:, nev:, nev:]
        imag = gram[:, :nev, nev:] - gram[:, nev:, :nev]
        partials.append(jnp.concatenate([real, imag], axis=2))
    partial_value = jnp.stack(partials, axis=1)
    tdev = partial_value.shape[0]
    rows = nev // slabs
    local_times = lax.axis_index("snk") * tdev + jnp.arange(tdev, dtype=jnp.int32)
    slab_part = lax.psum_scatter(partial_value, "slab", scatter_dimension=2, tiled=True)
    share = lax.psum_scatter(slab_part, "src", scatter_dimension=2, tiled=True).astype(BF16)
    sink = lax.all_gather(share, "src", axis=2, tiled=True)
    selector = (source_times[:, None] == local_times[None, :]).astype(BF16)
    term = jnp.dot(selector, sink.reshape(tdev, -1), preferred_element_type=F32)
    picked = lax.psum(term.astype(BF16), "snk")
    picked = picked.reshape((source_times.shape[0],) + sink.shape[1:])
    source = lax.all_gather(picked, "slab", axis=2, tiled=True)
    stacked = jnp.concatenate([sink[..., :nev], sink[..., nev:]], axis=2)
    prod = jnp.einsum("tmra,tsqab->mtsqrb", stacked, perambulator, preferred_element_type=F32)
    creal = prod[..., :rows, :nev] - prod[..., rows:, nev:]
    cimag = prod[..., :rows, nev:] + prod[..., rows:, :nev]
    half = jnp.concatenate([creal, cimag], axis=4).astype(BF16)
    both = jnp.concatenate([source[..., :nev], source[..., nev:]], axis=2)
    quad = jnp.einsum("mtsqrb,smcb->mtsqrc", half, both, preferred_element_type=F32)
    dreal = quad[..., :rows, :nev] + quad[..., rows:, nev:]
    dimag = quad[..., rows:, :nev] - quad[..., :rows, nev:]
    return jnp.concatenate([dreal, dimag], axis=-1)


def turned(x, nev):
    return jnp.concatenate([x[:, nev:], -x[:, :nev]], axis=1)


def circle(f):
    turns = jnp.floor(4.0 * f + 0.5)
    r = (f - 0.25 * turns) * (2.0 * math.pi)
    n = turns.astype(jnp.int32) & 3
    x = r * r
    c = 1.0 + x * (-1 / 2 + x * (1 / 24 + x * (-1 / 720 + x * (1 / 40320))))
    s = r * (1.0 + x * (-1 / 6 + x * (1 / 120 + x * (-1 / 5040 + x * (1 / 362880)))))
    odd = (n & 1) == 1
    cosine = jnp.where(odd, s, c)
    sine = jnp.where(odd, c, s)
    return (
        jnp.where((n == 1) | (n == 2), -cosine, cosine),
        jnp.where(n >= 2, -sine, sine),
    )


def phase(tab, i, y, core, width):
    cy = jnp.broadcast_to(tab[2 + 2 * core, i, pl.ds(y, 1), :], (LX, 128))
    sy = jnp.broadcast_to(tab[3 + 2 * core, i, pl.ds(y, 1), :], (LX, 128))
    cx, sx = tab[0, i], tab[1, i]
    c = cx * cy - sx * sy
    s = sx * cy + cx * sy
    return [jnp.concatenate([x] * (width // 128), axis=1) for x in (c, s)]


def site_sums(pieces, vec, tab, core, wide, lhs, sums):
    count, width = vec.shape
    nev = width // 2
    chunk = min(count, CHUNK)

    def spread(c):
        for y in range(c * chunk // LX, (c + 1) * chunk // LX):
            at = pl.ds(y * LX, LX)
            v = vec[at, :].astype(F32)
            u = turned(v, nev)
            for i, k in enumerate(pieces):
                c_, s_ = phase(tab, k, y, core, width)
                wide[at, i * width : (i + 1) * width] = (c_ * v + s_ * u).astype(BF16)

    spread(0)
    for c in range(count // chunk):
        at = slice(c * chunk, (c + 1) * chunk)
        for i in range(len(pieces)):
            g = jnp.dot(
                lhs[:, at], wide[at, i * width : (i + 1) * width], preferred_element_type=F32
            )
            sums[i] = g if c == 0 else sums[i] + g
        if (c + 1) * chunk < count:
            spread(c + 1)


def own_kernel(nsrc, slabs, lz, pieces, mom_hbm, eig_hbm, acc_ref, tab, vec, *refs):
    mom_ref, wide, tran, sums, mom_sem, sem = refs
    nev = vec.shape[1] // 2
    slab = lax.axis_index("slab")
    src = lax.axis_index("src")
    small = pltpu.make_async_copy(mom_hbm, mom_ref, mom_sem)
    small.start()
    copy = pltpu.make_async_copy(eig_hbm.at[slab], vec, sem)
    copy.start()
    small.wait()
    index = lax.broadcasted_iota(jnp.int32, (LX, 128), 0)
    for k in range(nsrc):
        mom = mom_ref[pl.ds(src ^ k, 1), :]
        px, py, pz = (jnp.broadcast_to(mom[:, i : i + 1], (LX, 128)) for i in range(3))
        tab[0, k], tab[1, k] = circle((px * index % LX).astype(F32) / LX)
        for core in range(2):
            z = src * slabs + (1 - slab if core else slab)
            fz = (pz * z % lz).astype(F32) / lz
            fy = (py * index % LY).astype(F32) / LY
            tab[2 + 2 * core, k], tab[3 + 2 * core, k] = circle(fy + fz)
    copy.wait()
    tran[...] = vec[...].T
    site_sums(pieces, vec, tab, 0, wide, tran, sums)
    for i in range(len(pieces)):
        acc_ref[i] = sums[i, :nev] + turned(sums[i, nev:], nev)


def same_kernel(pieces, times_hbm, eig_ref, tab, acc_ref, *refs):
    n = len(pieces)
    same = refs[:n]
    wide, rest, times_ref, tran, lhs, sums, sem = refs[n:]
    copy = pltpu.make_async_copy(times_hbm, times_ref, sem)
    copy.start()
    width = eig_ref.shape[2]
    nev = width // 2
    rows = nev // 2
    slab = lax.axis_index("slab")
    vec = eig_ref.at[slab]
    tran[...] = vec[...].T
    for i in range(2):
        lower = tran[i * nev : i * nev + rows, :]
        upper = tran[i * nev + rows : (i + 1) * nev, :]
        lhs[i * rows : (i + 1) * rows, :] = jnp.where(slab == 0, lower, upper)
        rest[i * rows : (i + 1) * rows, :] = jnp.where(slab == 0, upper, lower)
    site_sums(pieces, vec, tab, 1, wide, lhs, sums)
    copy.wait()
    for i, k in enumerate(pieces):
        e = sums[i, :rows] + turned(sums[i, rows:], nev)
        e = e + jnp.where(slab == 0, acc_ref[i, :rows], acc_ref[i, rows:])
        same[i][:rows, :] = e.astype(same[i].dtype)
        if k:
            for s in range(times_ref.shape[1]):
                time = jnp.broadcast_to(times_ref[:, s : s + 1].astype(F32), (TAIL, width))
                same[i][rows + s * TAIL : rows + (s + 1) * TAIL, :] = time.astype(BF16)


def cross_kernel(wide, rest, acc_ref, *outs):
    rows, width = outs[0].shape
    nev = width // 2
    slab = lax.axis_index("slab")
    for i, out in enumerate(outs):
        g = jnp.dot(rest[...], wide[:, i * width : (i + 1) * width], preferred_element_type=F32)
        e = g[:rows] + turned(g[rows:], nev)
        e = e + jnp.where(slab == 0, acc_ref[i, rows:], acc_ref[i, :rows])
        out[...] = e.astype(out.dtype)


def sum_kernel(own, *refs):
    out = refs[-1]
    rows = out.shape[0]
    total = own[...]
    for r in refs[:-1]:
        total = total + r[:rows, :].astype(F32)
    out[...] = total.astype(BF16)


def both_kernel(own, *refs):
    done = refs[-3]
    out, both = refs[-2:]
    total = own[...]
    for r in refs[:-3]:
        total = total + r[...].astype(F32)
    red = total.astype(BF16)
    out[...] = red
    slab = lax.axis_index("slab")
    both[0] = jnp.where(slab == 0, done[...], red)
    both[1] = jnp.where(slab == 0, red, done[...])


def pick_kernel(nsrc, labels, chained, times_ref, *refs):
    n = len(labels)
    sent = refs[: nsrc - 1]
    seen = refs[nsrc - 1 : nsrc - 1 + n]
    before = refs[nsrc - 1 + n : -nsrc]
    outs = refs[-nsrc:]
    rows, width = seen[0].shape[-2:]
    snk = lax.axis_index("snk")
    slab = lax.axis_index("slab")
    for k in range(nsrc):
        for s in range(outs[k].shape[0]):
            if k == 0:
                want = jnp.full((TAIL, 128), times_ref[s].astype(F32), F32)
            else:
                want = sent[k - 1][rows + s * TAIL : rows + (s + 1) * TAIL, :128].astype(F32)
            mask = []
            for d, other in labels:
                parts = (0, 1) if other is None else (1 - slab if other else slab,)
                for part in parts:
                    time = ((snk ^ d) * 2 + part).astype(F32)
                    one = (want == time).astype(F32).astype(BF16)
                    mask.append(jnp.concatenate([one] * (width // 128), axis=1))
            for r in range(rows // TAIL):
                at = slice(r * TAIL, (r + 1) * TAIL)
                total = before[k][s, at, :] if chained else None
                views = []
                for (_, other), x in zip(labels, seen):
                    views += [x[at, :]] if other is not None else [x[0, at, :], x[1, at, :]]
                for one, x in zip(mask, views):
                    term = one * x
                    total = term if total is None else total + term
                outs[k][s, at, :] = total


def half_kernel(pieces, *refs):
    sinks = refs[:pieces]
    per_ref = refs[pieces]
    outs = refs[pieces + 1 : 2 * pieces + 1]
    lhs, rhs = refs[2 * pieces + 1 :]
    tdev, rows, width = sinks[0].shape
    nev = width // 2
    sdev, nq = per_ref.shape[1:3]
    for t in range(tdev):
        for k in range(pieces):
            lhs[t, k * rows : (k + 1) * rows, :] = sinks[k][t]
        for s in range(sdev):
            for q in range(nq):
                p = per_ref[t, s, q]
                rhs[s, :nev, q * width : (q + 1) * width] = p
                rhs[s, nev:, q * width : (q + 1) * width] = (-turned(p.astype(F32), nev)).astype(BF16)
            h = jnp.dot(lhs[t], rhs[s], preferred_element_type=F32).astype(BF16)
            for q in range(nq):
                for k in range(pieces):
                    part = h[k * rows : (k + 1) * rows, q * width : (q + 1) * width]
                    outs[k][s, t * nq + q] = part


def block_kernel(pieces, chained, *refs):
    n = len(pieces)
    half, mine, other = refs[:n], refs[n : 2 * n], refs[2 * n : 3 * n]
    out_hbm, rhs, buf, sem = refs[3 * n + chained :]
    sdev, rows, width = mine[0].shape
    nev = width // 2
    tdev, nq = buf.shape[1:3]
    slab = lax.axis_index("slab")
    src = lax.axis_index("src")
    copies = []
    for j, k in enumerate(pieces):
        for s in range(sdev):
            slot, part = j * sdev + s, s % 2
            lower = jnp.where(slab == 0, mine[j][s], other[j][s])
            upper = jnp.where(slab == 0, other[j][s], mine[j][s])
            for at, x in ((0, lower), (rows, upper)):
                rhs[part, at : at + rows, :] = x
                rhs[part, nev + at : nev + at + rows, :] = (-turned(x.astype(F32), nev)).astype(BF16)
            out = lax.dot_general(
                half[j][s].reshape(tdev * nq * rows, width),
                rhs[part],
                (((1,), (1,)), ((), ())),
                preferred_element_type=F32,
            )
            buf[slot] = out.reshape(tdev, nq, rows, width)
            for t in range(tdev):
                copies.append(
                    pltpu.make_async_copy(
                        buf.at[slot, t], out_hbm.at[src ^ k, t, s], sem.at[slot, t]
                    )
                )
                copies[-1].start()
    for copy in copies:
        copy.wait()


def fast(eigvecs, perambulator, momenta, source_times):
    nsrc, nsnk, slabs = (lax.axis_size(a) for a in ("src", "snk", "slab"))
    tdev, count, width = eigvecs.shape
    sdev = source_times.shape[0]
    nq = perambulator.shape[2]
    nev = width // 2
    rows = nev // slabs
    lz = count // (LX * LY) * nsrc * slabs

    def shape(dims, dtype=BF16):
        return jax.ShapeDtypeStruct(dims, dtype)

    def params(mib):
        return pltpu.CompilerParams(vmem_limit_bytes=mib * 2**20)

    def cost(flops, moved):
        return pl.CostEstimate(flops=flops, bytes_accessed=moved, transcendentals=0)

    def swap(x):
        return lax.ppermute(x, "slab", [(0, 1), (1, 0)])

    def cross(x, k):
        return lax.ppermute(x, "src", [(i, i ^ k) for i in range(nsrc)])

    def far(x, k):
        pairs = [(2 * i + j, 2 * (i ^ k) + 1 - j) for i in range(nsrc) for j in range(2)]
        return lax.ppermute(x, ("src", "slab"), pairs)

    def along(x, d):
        return lax.ppermute(x, "snk", [(i, i ^ d) for i in range(nsnk)])

    theirs = swap(eigvecs)
    work = 2 * width * count * width
    hbm = pl.BlockSpec(memory_space=pltpu.HBM)
    sent = list(range(nsrc - 1, -1, -1))

    def grams(n):
        return [
            pltpu.VMEM((count, n * width), BF16),
            pltpu.VMEM((width, count), BF16),
            pltpu.VMEM((n, width, width), F32),
        ]

    vec = pltpu.VMEM((count, width), BF16)
    sem = pltpu.SemaphoreType.DMA

    def held(x):
        return pltpu.with_memory_space_constraint(x, pltpu.HBM)

    eigs = held(eigvecs)
    acc, tab = pl.pallas_call(
        functools.partial(own_kernel, nsrc, slabs, lz, sent),
        out_shape=[shape((len(sent), nev, width), F32), shape((6, nsrc, LX, 128), F32)],
        in_specs=[hbm, hbm],
        out_specs=[VMEM] * 2,
        scratch_shapes=[vec, pltpu.VMEM(momenta.shape, jnp.int32)] + grams(len(sent)) + [sem] * 2,
        cost_estimate=cost(len(sent) * work, 2 * count * width),
        compiler_params=params(12),
        name="gram_own",
    )(held(momenta), eigs)
    parts = pl.pallas_call(
        functools.partial(same_kernel, sent),
        out_shape=[shape((rows + sdev * TAIL, width)) if k else shape((rows, width), F32) for k in sent]
        + [shape((count, nsrc * width)), shape((2 * rows, count))],
        in_specs=[hbm] + [VMEM] * 3,
        out_specs=[VMEM] * (nsrc + 2),
        scratch_shapes=[
            pltpu.VMEM((1, sdev), jnp.int32),
            pltpu.VMEM((width, count), BF16),
            pltpu.VMEM((2 * rows, count), BF16),
            pltpu.VMEM((nsrc, 2 * rows, width), F32),
            sem,
        ],
        cost_estimate=cost(nsrc * work // 2, 2 * count * width),
        compiler_params=params(12),
        name="gram_same",
    )(held(source_times.reshape(1, sdev)), theirs, tab, acc)
    same = dict(zip(sent, parts))
    other = pl.pallas_call(
        cross_kernel,
        out_shape=[shape((rows, width), BF16 if k else F32) for k in sent],
        in_specs=[VMEM] * 3,
        out_specs=[VMEM] * nsrc,
        cost_estimate=cost(nsrc * work // 2, 2 * count * width),
        compiler_params=params(6),
        name="gram_cross",
    )(*parts[nsrc:], acc)
    other = dict(zip(sent, other))
    got = [cross(same[k], k) for k in range(1, nsrc)]
    more = [far(other[k], k) for k in range(1, nsrc)]
    red = pl.pallas_call(
        sum_kernel,
        out_shape=shape((rows, width)),
        in_specs=[VMEM] * nsrc,
        out_specs=VMEM,
        compiler_params=params(4),
        name="sum_same",
    )(same[0], *got)
    red_far, both = pl.pallas_call(
        both_kernel,
        out_shape=[shape((rows, width)), shape((tdev, rows, width))],
        in_specs=[VMEM] * (nsrc + 1),
        out_specs=[VMEM] * 2,
        compiler_params=params(4),
        name="sum_both",
    )(swap(other[0]), *more, red)
    views = {0: {0: red, 1: red_far}}
    seen = [((0, p), x) for p, x in views[0].items()]
    for bit in reversed([1 << i for i in range(nsnk.bit_length() - 1)]):
        for d in sorted(views):
            if bit == 1 and d == 0 and nsnk > 2:
                seen.append(((1, None), along(both, 1)))
                continue
            views[d | bit] = {p: along(x, bit) for p, x in views[d].items()}
            seen += [((d | bit, p), x) for p, x in views[d | bit].items()]
    labels, seen = zip(*seen)
    sinks = [both] + [cross(both, k) for k in range(1, nsrc)]

    def pick(which, before):
        return pl.pallas_call(
            functools.partial(pick_kernel, nsrc, [labels[i] for i in which], bool(before)),
            out_shape=[shape((sdev, rows, width))] * nsrc,
            in_specs=[SMEM] + [VMEM] * (nsrc - 1 + len(which) + len(before)),
            out_specs=[VMEM] * nsrc,
            compiler_params=params(8),
        )(source_times, *got, *(seen[i] for i in which), *before)

    late = len(labels) - 1
    picked = pick(list(range(late)), [])
    picked = pick([late], picked)

    tq = tdev * nq

    def halves(which):
        n = len(which)
        out = pl.pallas_call(
            functools.partial(half_kernel, n),
            out_shape=[shape((sdev, tq, rows, width))] * n,
            in_specs=[VMEM] * (n + 1),
            out_specs=[VMEM] * n,
            scratch_shapes=[
                pltpu.VMEM((tdev, n * rows, width), BF16),
                pltpu.VMEM((sdev, width, nq * width), BF16),
            ],
            cost_estimate=cost(2 * tq * sdev * n * rows * width * width, 2 * perambulator.size),
            compiler_params=params(12),
        )(*(sinks[k] for k in which), perambulator)
        return dict(zip(which, out))

    half = halves(list(range(nsrc)))

    mine = [picked[0]] + [cross(picked[k], k) for k in range(1, nsrc)]
    other = [swap(x) for x in mine]

    def finish(which, before):
        n = len(which)
        chained = before is not None
        return pl.pallas_call(
            functools.partial(block_kernel, which, chained),
            out_shape=shape((nsrc, tdev, sdev, nq, rows, width), F32),
            in_specs=[VMEM] * (3 * n) + [hbm] * chained,
            out_specs=hbm,
            scratch_shapes=[
                pltpu.VMEM((2, width, width), BF16),
                pltpu.VMEM((n * sdev, tdev, nq, rows, width), F32),
                pltpu.SemaphoreType.DMA((n * sdev, tdev)),
            ],
            input_output_aliases={3 * n: 0} if chained else {},
            cost_estimate=cost(
                2 * n * tq * sdev * rows * width * width, 4 * n * tq * sdev * rows * width
            ),
            compiler_params=params(16),
        )(
            *(x[k] for x in (half, mine, other) for k in which),
            *([before] if chained else []),
        )

    blocks = finish([0], None)
    return finish(list(range(1, nsrc)), blocks)


def local(eigvecs, perambulator, momenta, source_times):
    nsrc = lax.axis_size("src")
    fits = (
        lax.axis_size("slab") == 2
        and momenta.shape[0] == nsrc
        and nsrc & (nsrc - 1) == 0
        and lax.axis_size("snk") & (lax.axis_size("snk") - 1) == 0
        and eigvecs.shape[0] == 2
        and eigvecs.shape[1] == LX * LY
        and source_times.shape[0] == eigvecs.shape[0]
    )
    return (fast if fits else general)(eigvecs, perambulator, momenta, source_times)


def solution(mesh):
    placed = (P("snk", ("src", "slab"), None), P("snk", "src", None, None, None), P(), P("src"))

    return jax.shard_map(
        local,
        mesh=mesh,
        in_specs=placed,
        out_specs=P(None, "snk", "src", None, "slab", None),
        check_vma=False,
    )
```

profile of v0, /device:TPU:0, one launch (start us, length us, event | category | flops | bytes accessed | tf_op | source)
XLA Modules:
  0.0 54.5 jit_solution(7816063412790623602)
XLA Ops:
  0.5 4.0 %gram_own.1 = (f32[4,192,384]{2,1,0:T(8,128)S(1)}, f32[6,4,32,128]{3,2,1,0:T(8,128)S(1)}) custom-call(s32[4,3]{1,0:T(4,128)} %mom_hbm.1, bf16[2,1024,384]{2,1,0:T(8,128)(2,1)} %eig_hbm.1), custom_call_target="tpu_custom_call" | custom-call | flops 1207959552 | bytes 786432 | tf_op jit(solution)/shard_map/gram_own/pallas_call | solution.py:364
  4.5 2.9 %gram_same.1 = (bf16[128,384]{1,0:T(8,128)(2,1)S(1)}, bf16[128,384]{1,0:T(8,128)(2,1)S(1)}, bf16[128,384]{1,0:T(8,128)(2,1)S(1)}, f32[96,384]{1,0:T(8,128)S(1)},...) custom-call(s32[1,2]{1,0:T(1,128)} %bitcast.1, bf16[2,1024,384]{2,1,0:T(8,128)(2,1)S(1)} %collective-permute-done.eig_ref, ...), custom_call_target="tpu_custom_call" | custom-call | flops 603979776 | bytes 786432 | tf_op jit(solution)/shard_map/gram_same/pallas_call | solution.py:374
  7.4 2.5 %collective-permute-start.5 = (bf16[128,384]{1,0:T(8,128)(2,1)S(1)}, bf16[128,384]{1,0:T(8,128)(2,1)S(1)}, u32[]{:S(2)}, u32[]{:S(2)}) collective-permute-start(bf16[128,384]{1,0:T(8,128)(2,1)S(1)} %get-tuple-element.40), channel_id=1, source_target_pairs={{0,8},{8,0},{16,24},{24,16},{1,9},{9,1},{17,25},{25,17},{2,10},{10... | collective-permute-start | bytes 294920 | tf_op jit(solution)/shard_map/ppermute | solution.py:336
  10.0 1.5 %collective-permute-start.6 = (bf16[128,384]{1,0:T(8,128)(2,1)S(1)}, bf16[128,384]{1,0:T(8,128)(2,1)S(1)}, u32[]{:S(2)}, u32[]{:S(2)}) collective-permute-start(bf16[128,384]{1,0:T(8,128)(2,1)S(1)} %get-tuple-element.41), channel_id=1, source_target_pairs={{0,16},{8,24},{16,0},{24,8},{1,17},{9,25},{17,1},{25,9},{2,18},{10... | collective-permute-start | bytes 294920 | tf_op jit(solution)/shard_map/ppermute | solution.py:336
  11.5 1.1 %gram_cross.1 = (bf16[96,384]{1,0:T(8,128)(2,1)S(1)}, bf16[96,384]{1,0:T(8,128)(2,1)S(1)}, bf16[96,384]{1,0:T(8,128)(2,1)S(1)}, f32[96,384]{1,0:T(8,128)S(1)}) custom-call(bf16[1024,1536]{1,0:T(8,128)(2,1)S(1)} %get-tuple-element.33.wide, bf16[192,1024]{1,0:T(8,128)(2,1)S(1)} %get-tuple-element.34.rest, f32[4,192,384]{2,1,0:T(8,128)S(1)} %get-tuple-element.32.acc_ref), custom_call_target="tpu_custom_call" | custom-call | flops 603979776 | bytes 786432 | tf_op jit(solution)/shard_map/gram_cross/pallas_call | solution.py:392
  12.9 1.6 %collective-permute-start.2 = (bf16[96,384]{1,0:T(8,128)(2,1)S(1)}, bf16[96,384]{1,0:T(8,128)(2,1)S(1)}, u32[]{:S(2)}, u32[]{:S(2)}) collective-permute-start(bf16[96,384]{1,0:T(8,128)(2,1)S(1)} %get-tuple-element.36), channel_id=1, source_target_pairs={{0,9},{1,8},{8,1},{9,0},{16,25},{17,24},{24,17},{25,16},{2,11},{3,... | collective-permute-start | bytes 221192 | tf_op jit(solution)/shard_map/ppermute | solution.py:340
  14.4 1.5 %collective-permute-start.3 = (bf16[96,384]{1,0:T(8,128)(2,1)S(1)}, bf16[96,384]{1,0:T(8,128)(2,1)S(1)}, u32[]{:S(2)}, u32[]{:S(2)}) collective-permute-start(bf16[96,384]{1,0:T(8,128)(2,1)S(1)} %get-tuple-element.37), channel_id=1, source_target_pairs={{0,17},{1,16},{8,25},{9,24},{16,1},{17,0},{24,9},{25,8},{2,19},{3,... | collective-permute-start | bytes 221192 | tf_op jit(solution)/shard_map/ppermute | solution.py:340
  16.4 2.9 %collective-permute-done.7.refs_2_ = bf16[128,384]{1,0:T(8,128)(2,1)S(1)} collective-permute-done((bf16[128,384]{1,0:T(8,128)(2,1)S(1)}, bf16[128,384]{1,0:T(8,128)(2,1)S(1)}, u32[]{:S(2)}, u32[]{:S(2)}) %collective-permute-start.7) | collective-permute-done | bytes 98336 | tf_op jit(solution)/shard_map/ppermute | solution.py:336
  19.3 2.7 %collective-permute-start.13 = (bf16[96,384]{1,0:T(8,128)(2,1)S(1)}, bf16[96,384]{1,0:T(8,128)(2,1)S(1)}, u32[]{:S(2)}, u32[]{:S(2)}) collective-permute-start(bf16[96,384]{1,0:T(8,128)(2,1)S(1)} %sum_same.1.refs_3_), channel_id=1, source_target_pairs={{0,4},{2,6},{4,0},{6,2},{1,5},{3,7},{5,1},{7,3},{8,12},{10,14},{12... | collective-permute-start | bytes 221192 | tf_op jit(solution)/shard_map/ppermute | solution.py:343
  22.1 1.6 %collective-permute-start.14 = (bf16[2,96,384]{2,1,0:T(8,128)(2,1)S(1)}, bf16[2,96,384]{2,1,0:T(8,128)(2,1)S(1)}, u32[]{:S(2)}, u32[]{:S(2)}) collective-permute-start(bf16[2,96,384]{2,1,0:T(8,128)(2,1)S(1)} %get-tuple-element.43.refs_0_), channel_id=1, source_target_pairs={{0,2},{2,0},{4,6},{6,4},{1,3},{3,1},{5,7},{7,5},{8,10},{10,8},{12,... | collective-permute-start | bytes 442376 | tf_op jit(solution)/shard_map/ppermute | solution.py:343
  23.7 2.0 %collective-permute-start.11 = (bf16[96,384]{1,0:T(8,128)(2,1)S(1)}, bf16[96,384]{1,0:T(8,128)(2,1)S(1)}, u32[]{:S(2)}, u32[]{:S(2)}) collective-permute-start(bf16[96,384]{1,0:T(8,128)(2,1)S(1)} %get-tuple-element.47.refs_4_), channel_id=1, source_target_pairs={{0,4},{2,6},{4,0},{6,2},{1,5},{3,7},{5,1},{7,3},{8,12},{10,14},{12... | collective-permute-start | bytes 221192 | tf_op jit(solution)/shard_map/ppermute | solution.py:343
  26.7 2.7 %collective-permute-done.11.refs_6_ = bf16[96,384]{1,0:T(8,128)(2,1)S(1)} collective-permute-done((bf16[96,384]{1,0:T(8,128)(2,1)S(1)}, bf16[96,384]{1,0:T(8,128)(2,1)S(1)}, u32[]{:S(2)}, u32[]{:S(2)}) %collective-permute-start.11) | collective-permute-done | bytes 73760 | tf_op jit(solution)/shard_map/ppermute | solution.py:343
  29.4 3.0 %collective-permute-start.12 = (bf16[96,384]{1,0:T(8,128)(2,1)S(1)}, bf16[96,384]{1,0:T(8,128)(2,1)S(1)}, u32[]{:S(2)}, u32[]{:S(2)}) collective-permute-start(bf16[96,384]{1,0:T(8,128)(2,1)S(1)} %collective-permute-done.11.refs_6_), channel_id=1, source_target_pairs={{0,2},{2,0},{4,6},{6,4},{1,3},{3,1},{5,7},{7,5},{8,10},{10,8},{12,... | collective-permute-start | bytes 221192 | tf_op jit(solution)/shard_map/ppermute | solution.py:343
  33.0 1.0 %shard_map.47 = (bf16[2,96,384]{2,1,0:T(8,128)(2,1)S(1)}, bf16[2,96,384]{2,1,0:T(8,128)(2,1)S(1)}, bf16[2,96,384]{2,1,0:T(8,128)(2,1)S(1)}, bf16[2,96,384]{2,1,0:T(8,128)(2,1)S(1)}) custom-call(s32[2]{0:T(128)S(1)} %copy-done, bf16[128,384]{1,0:T(8,128)(2,1)S(1)} %collective-permute-done.5.refs_0_, bf16[128,384]{1,0:T(8,128)(2,1)S(1)} %collective-permute-done.6.refs_1_, ...), custom_call_target="tpu_custom_call" | custom-call | tf_op jit(solution)/shard_map/pallas_call | solution.py:433
  34.0 0.7 %collective-permute-done.12.refs_3_ = bf16[96,384]{1,0:T(8,128)(2,1)S(1)} collective-permute-done((bf16[96,384]{1,0:T(8,128)(2,1)S(1)}, bf16[96,384]{1,0:T(8,128)(2,1)S(1)}, u32[]{:S(2)}, u32[]{:S(2)}) %collective-permute-start.12) | collective-permute-done | bytes 73760 | tf_op jit(solution)/shard_map/ppermute | solution.py:343
  36.0 0.7 %collective-permute-start.17 = (bf16[2,96,384]{2,1,0:T(8,128)(2,1)S(1)}, bf16[2,96,384]{2,1,0:T(8,128)(2,1)S(1)}, u32[]{:S(2)}, u32[]{:S(2)}) collective-permute-start(bf16[2,96,384]{2,1,0:T(8,128)(2,1)S(1)} %get-tuple-element.53), channel_id=1, source_target_pairs={{0,16},{8,24},{16,0},{24,8},{1,17},{9,25},{17,1},{25,9},{2,18},{10... | collective-permute-start | bytes 442376 | tf_op jit(solution)/shard_map/ppermute | solution.py:336
  36.7 2.3 %collective-permute-start.18 = (bf16[2,96,384]{2,1,0:T(8,128)(2,1)S(1)}, bf16[2,96,384]{2,1,0:T(8,128)(2,1)S(1)}, u32[]{:S(2)}, u32[]{:S(2)}) collective-permute-start(bf16[2,96,384]{2,1,0:T(8,128)(2,1)S(1)} %get-tuple-element.54), channel_id=1, source_target_pairs={{0,24},{8,16},{16,8},{24,0},{1,25},{9,17},{17,9},{25,1},{2,26},{10... | collective-permute-start | bytes 442376 | tf_op jit(solution)/shard_map/ppermute | solution.py:336
  39.5 0.9 %collective-permute-done.9.refs_2_ = bf16[2,96,384]{2,1,0:T(8,128)(2,1)S(1)} collective-permute-done((bf16[2,96,384]{2,1,0:T(8,128)(2,1)S(1)}, bf16[2,96,384]{2,1,0:T(8,128)(2,1)S(1)}, u32[]{:S(2)}, u32[]{:S(2)}) %collective-permute-start.9) | collective-permute-done | bytes 147488 | tf_op jit(solution)/shard_map/ppermute | solution.py:336
  40.4 1.8 %collective-permute-done.16.refs_3_ = bf16[2,96,384]{2,1,0:T(8,128)(2,1)S(1)} collective-permute-done((bf16[2,96,384]{2,1,0:T(8,128)(2,1)S(1)}, bf16[2,96,384]{2,1,0:T(8,128)(2,1)S(1)}, u32[]{:S(2)}, u32[]{:S(2)}) %collective-permute-start.16) | collective-permute-done | bytes 147488 | tf_op jit(solution)/shard_map/ppermute | solution.py:336
  42.7 1.7 %collective-permute-done.18.refs_5_ = bf16[2,96,384]{2,1,0:T(8,128)(2,1)S(1)} collective-permute-done((bf16[2,96,384]{2,1,0:T(8,128)(2,1)S(1)}, bf16[2,96,384]{2,1,0:T(8,128)(2,1)S(1)}, u32[]{:S(2)}, u32[]{:S(2)}) %collective-permute-start.18) | collective-permute-done | bytes 147488 | tf_op jit(solution)/shard_map/ppermute | solution.py:336
  44.4 1.1 %collective-permute-done.8.refs_1_ = bf16[2,96,384]{2,1,0:T(8,128)(2,1)S(1)} collective-permute-done((bf16[2,96,384]{2,1,0:T(8,128)(2,1)S(1)}, bf16[2,96,384]{2,1,0:T(8,128)(2,1)S(1)}, u32[]{:S(2)}, u32[]{:S(2)}) %collective-permute-start.8) | collective-permute-done | bytes 147488 | tf_op jit(solution)/shard_map/ppermute | solution.py:336
  45.5 2.7 %shard_map.46 = (bf16[2,8,96,384]{3,2,1,0:T(8,128)(2,1)S(1)}, bf16[2,8,96,384]{3,2,1,0:T(8,128)(2,1)S(1)}, bf16[2,8,96,384]{3,2,1,0:T(8,128)(2,1)S(1)}, bf16[2,8,96,384]{3,2,1,0:T(8,128)(2,1)S(1)}) custom-call(bf16[2,96,384]{2,1,0:T(8,128)(2,1)S(1)} %get-tuple-element.43.refs_0_, bf16[2,96,384]{2,1,0:T(8,128)(2,1)S(1)} %collective-permute-done.8.refs_1_, ...), custom_call_target="tpu_custom_call" | custom-call | flops 1811939328 | bytes 2359296 | tf_op jit(solution)/shard_map/pallas_call | solution.py:449
  48.3 2.3 %shard_map.49.refs_9_ = f32[4,2,2,4,96,384]{5,4,3,2,1,0:T(8,128)} custom-call(bf16[2,8,96,384]{3,2,1,0:T(8,128)(2,1)S(1)} %get-tuple-element.55.refs_0_, bf16[2,96,384]{2,1,0:T(8,128)(2,1)S(1)} %get-tuple-element.56.refs_1_, bf16[2,96,384]{2,1,0:T(8,128)(2,1)S(1)} %collective-permute-done.22.refs_2_), custom_call_target="tpu_custom_call" | custom-call | flops 452984832 | bytes 2359296 | tf_op jit(solution)/shard_map/pallas_call | solution.py:471
  50.6 3.7 %shard_map.50 = f32[4,2,2,4,96,384]{5,4,3,2,1,0:T(8,128)} custom-call(bf16[2,8,96,384]{3,2,1,0:T(8,128)(2,1)S(1)} %get-tuple-element.44.refs_0_, bf16[2,8,96,384]{3,2,1,0:T(8,128)(2,1)S(1)} %get-tuple-element.45.refs_1_, bf16[2,8,96,384]{3,2,1,0:T(8,128)(2,1)S(1)} %get-tuple-element.46.refs_2_, ...), custom_call_target="tpu_custom_call", output_to_operand_aliasing={{}: (9, {})} | custom-call | flops 1358954496 | bytes 7077888 | tf_op jit(solution)/shard_map/pallas_call | solution.py:471
  (36 shorter events, 5.3 us)
Async XLA Ops:
  0.0 4.5 %collective-permute-start = (bf16[2,1024,384]{2,1,0:T(8,128)(2,1)}, bf16[2,1024,384]{2,1,0:T(8,128)(2,1)S(1)}, u32[]{:S(2)}, u32[]{:S(2)}) collective-permute-start(bf16[2,1024,384]{2,1,0:T(8,128)(2,1)} %eig_hbm.1), channel_id=1, source_target_pairs={{0,1},{1,0},{2,3},{3,2},{4,5},{5,4},{6,7},{7,6},{8,9},{9,8},{10,11... | collective-permute-start | bytes 4718600 | tf_op jit(solution)/shard_map/ppermute | solution.py:333
  7.4 7.0 %collective-permute-start.5 = (bf16[128,384]{1,0:T(8,128)(2,1)S(1)}, bf16[128,384]{1,0:T(8,128)(2,1)S(1)}, u32[]{:S(2)}, u32[]{:S(2)}) collective-permute-start(bf16[128,384]{1,0:T(8,128)(2,1)S(1)} %get-tuple-element.40), channel_id=1, source_target_pairs={{0,8},{8,0},{16,24},{24,16},{1,9},{9,1},{17,25},{25,17},{2,10},{10... | collective-permute-start | bytes 294920 | tf_op jit(solution)/shard_map/ppermute | solution.py:336
  10.0 6.0 %collective-permute-start.6 = (bf16[128,384]{1,0:T(8,128)(2,1)S(1)}, bf16[128,384]{1,0:T(8,128)(2,1)S(1)}, u32[]{:S(2)}, u32[]{:S(2)}) collective-permute-start(bf16[128,384]{1,0:T(8,128)(2,1)S(1)} %get-tuple-element.41), channel_id=1, source_target_pairs={{0,16},{8,24},{16,0},{24,8},{1,17},{9,25},{17,1},{25,9},{2,18},{10... | collective-permute-start | bytes 294920 | tf_op jit(solution)/shard_map/ppermute | solution.py:336
  12.5 33.0 %copy-start.1 = (bf16[2,2,4,192,384]{4,3,2,1,0:T(8,128)(2,1)S(1)}, bf16[2,2,4,192,384]{4,3,2,1,0:T(8,128)(2,1)}, u32[]{:S(2)}) copy-start(bf16[2,2,4,192,384]{4,3,2,1,0:T(8,128)(2,1)} %refs_4_.1) | copy-start | bytes 7077892
  12.6 9.4 %collective-permute-start.1 = (f32[96,384]{1,0:T(8,128)S(1)}, f32[96,384]{1,0:T(8,128)S(1)}, u32[]{:S(2)}, u32[]{:S(2)}) collective-permute-start(f32[96,384]{1,0:T(8,128)S(1)} %get-tuple-element.35), channel_id=1, source_target_pairs={{0,1},{1,0},{2,3},{3,2},{4,5},{5,4},{6,7},{7,6},{8,9},{9,8},{10,11... | collective-permute-start | bytes 442376 | tf_op jit(solution)/shard_map/ppermute | solution.py:333
  12.6 6.6 %collective-permute-start.7 = (bf16[128,384]{1,0:T(8,128)(2,1)S(1)}, bf16[128,384]{1,0:T(8,128)(2,1)S(1)}, u32[]{:S(2)}, u32[]{:S(2)}) collective-permute-start(bf16[128,384]{1,0:T(8,128)(2,1)S(1)} %get-tuple-element.42), channel_id=1, source_target_pairs={{0,24},{8,16},{16,8},{24,0},{1,25},{9,17},{17,9},{25,1},{2,26},{10... | collective-permute-start | bytes 294920 | tf_op jit(solution)/shard_map/ppermute | solution.py:336
  12.9 9.1 %collective-permute-start.2 = (bf16[96,384]{1,0:T(8,128)(2,1)S(1)}, bf16[96,384]{1,0:T(8,128)(2,1)S(1)}, u32[]{:S(2)}, u32[]{:S(2)}) collective-permute-start(bf16[96,384]{1,0:T(8,128)(2,1)S(1)} %get-tuple-element.36), channel_id=1, source_target_pairs={{0,9},{1,8},{8,1},{9,0},{16,25},{17,24},{24,17},{25,16},{2,11},{3,... | collective-permute-start | bytes 221192 | tf_op jit(solution)/shard_map/ppermute | solution.py:340
  14.4 7.5 %collective-permute-start.3 = (bf16[96,384]{1,0:T(8,128)(2,1)S(1)}, bf16[96,384]{1,0:T(8,128)(2,1)S(1)}, u32[]{:S(2)}, u32[]{:S(2)}) collective-permute-start(bf16[96,384]{1,0:T(8,128)(2,1)S(1)} %get-tuple-element.37), channel_id=1, source_target_pairs={{0,17},{1,16},{8,25},{9,24},{16,1},{17,0},{24,9},{25,8},{2,19},{3,... | collective-permute-start | bytes 221192 | tf_op jit(solution)/shard_map/ppermute | solution.py:340
  15.9 6.1 %collective-permute-start.4 = (bf16[96,384]{1,0:T(8,128)(2,1)S(1)}, bf16[96,384]{1,0:T(8,128)(2,1)S(1)}, u32[]{:S(2)}, u32[]{:S(2)}) collective-permute-start(bf16[96,384]{1,0:T(8,128)(2,1)S(1)} %get-tuple-element.38), channel_id=1, source_target_pairs={{0,25},{1,24},{8,17},{9,16},{16,9},{17,8},{24,1},{25,0},{2,27},{3,... | collective-permute-start | bytes 221192 | tf_op jit(solution)/shard_map/ppermute | solution.py:340
  19.3 6.9 %collective-permute-start.13 = (bf16[96,384]{1,0:T(8,128)(2,1)S(1)}, bf16[96,384]{1,0:T(8,128)(2,1)S(1)}, u32[]{:S(2)}, u32[]{:S(2)}) collective-permute-start(bf16[96,384]{1,0:T(8,128)(2,1)S(1)} %sum_same.1.refs_3_), channel_id=1, source_target_pairs={{0,4},{2,6},{4,0},{6,2},{1,5},{3,7},{5,1},{7,3},{8,12},{10,14},{12... | collective-permute-start | bytes 221192 | tf_op jit(solution)/shard_map/ppermute | solution.py:343
  22.1 11.0 %collective-permute-start.14 = (bf16[2,96,384]{2,1,0:T(8,128)(2,1)S(1)}, bf16[2,96,384]{2,1,0:T(8,128)(2,1)S(1)}, u32[]{:S(2)}, u32[]{:S(2)}) collective-permute-start(bf16[2,96,384]{2,1,0:T(8,128)(2,1)S(1)} %get-tuple-element.43.refs_0_), channel_id=1, source_target_pairs={{0,2},{2,0},{4,6},{6,4},{1,3},{3,1},{5,7},{7,5},{8,10},{10,8},{12,... | collective-permute-start | bytes 442376 | tf_op jit(solution)/shard_map/ppermute | solution.py:343
  23.7 5.7 %collective-permute-start.11 = (bf16[96,384]{1,0:T(8,128)(2,1)S(1)}, bf16[96,384]{1,0:T(8,128)(2,1)S(1)}, u32[]{:S(2)}, u32[]{:S(2)}) collective-permute-start(bf16[96,384]{1,0:T(8,128)(2,1)S(1)} %get-tuple-element.47.refs_4_), channel_id=1, source_target_pairs={{0,4},{2,6},{4,0},{6,2},{1,5},{3,7},{5,1},{7,3},{8,12},{10,14},{12... | collective-permute-start | bytes 221192 | tf_op jit(solution)/shard_map/ppermute | solution.py:343
  25.7 13.3 %collective-permute-start.10 = (bf16[2,96,384]{2,1,0:T(8,128)(2,1)S(1)}, bf16[2,96,384]{2,1,0:T(8,128)(2,1)S(1)}, u32[]{:S(2)}, u32[]{:S(2)}) collective-permute-start(bf16[2,96,384]{2,1,0:T(8,128)(2,1)S(1)} %get-tuple-element.43.refs_0_), channel_id=1, source_target_pairs={{0,24},{8,16},{16,8},{24,0},{1,25},{9,17},{17,9},{25,1},{2,26},{10... | collective-permute-start | bytes 442376 | tf_op jit(solution)/shard_map/ppermute | solution.py:336
  26.3 6.8 %collective-permute-start.15 = (bf16[96,384]{1,0:T(8,128)(2,1)S(1)}, bf16[96,384]{1,0:T(8,128)(2,1)S(1)}, u32[]{:S(2)}, u32[]{:S(2)}) collective-permute-start(bf16[96,384]{1,0:T(8,128)(2,1)S(1)} %collective-permute-done.13.refs_5_), channel_id=1, source_target_pairs={{0,2},{2,0},{4,6},{6,4},{1,3},{3,1},{5,7},{7,5},{8,10},{10,8},{12,... | collective-permute-start | bytes 221192 | tf_op jit(solution)/shard_map/ppermute | solution.py:343
  29.4 5.4 %collective-permute-start.12 = (bf16[96,384]{1,0:T(8,128)(2,1)S(1)}, bf16[96,384]{1,0:T(8,128)(2,1)S(1)}, u32[]{:S(2)}, u32[]{:S(2)}) collective-permute-start(bf16[96,384]{1,0:T(8,128)(2,1)S(1)} %collective-permute-done.11.refs_6_), channel_id=1, source_target_pairs={{0,2},{2,0},{4,6},{6,4},{1,3},{3,1},{5,7},{7,5},{8,10},{10,8},{12,... | collective-permute-start | bytes 221192 | tf_op jit(solution)/shard_map/ppermute | solution.py:343
  32.4 8.0 %collective-permute-start.9 = (bf16[2,96,384]{2,1,0:T(8,128)(2,1)S(1)}, bf16[2,96,384]{2,1,0:T(8,128)(2,1)S(1)}, u32[]{:S(2)}, u32[]{:S(2)}) collective-permute-start(bf16[2,96,384]{2,1,0:T(8,128)(2,1)S(1)} %get-tuple-element.43.refs_0_), channel_id=1, source_target_pairs={{0,16},{8,24},{16,0},{24,8},{1,17},{9,25},{17,1},{25,9},{2,18},{10... | collective-permute-start | bytes 442376 | tf_op jit(solution)/shard_map/ppermute | solution.py:336
  35.4 6.8 %collective-permute-start.16 = (bf16[2,96,384]{2,1,0:T(8,128)(2,1)S(1)}, bf16[2,96,384]{2,1,0:T(8,128)(2,1)S(1)}, u32[]{:S(2)}, u32[]{:S(2)}) collective-permute-start(bf16[2,96,384]{2,1,0:T(8,128)(2,1)S(1)} %get-tuple-element.52), channel_id=1, source_target_pairs={{0,8},{8,0},{16,24},{24,16},{1,9},{9,1},{17,25},{25,17},{2,10},{10... | collective-permute-start | bytes 442376 | tf_op jit(solution)/shard_map/ppermute | solution.py:336
  36.0 6.3 %collective-permute-start.17 = (bf16[2,96,384]{2,1,0:T(8,128)(2,1)S(1)}, bf16[2,96,384]{2,1,0:T(8,128)(2,1)S(1)}, u32[]{:S(2)}, u32[]{:S(2)}) collective-permute-start(bf16[2,96,384]{2,1,0:T(8,128)(2,1)S(1)} %get-tuple-element.53), channel_id=1, source_target_pairs={{0,16},{8,24},{16,0},{24,8},{1,17},{9,25},{17,1},{25,9},{2,18},{10... | collective-permute-start | bytes 442376 | tf_op jit(solution)/shard_map/ppermute | solution.py:336
  36.7 7.7 %collective-permute-start.18 = (bf16[2,96,384]{2,1,0:T(8,128)(2,1)S(1)}, bf16[2,96,384]{2,1,0:T(8,128)(2,1)S(1)}, u32[]{:S(2)}, u32[]{:S(2)}) collective-permute-start(bf16[2,96,384]{2,1,0:T(8,128)(2,1)S(1)} %get-tuple-element.54), channel_id=1, source_target_pairs={{0,24},{8,16},{16,8},{24,0},{1,25},{9,17},{17,9},{25,1},{2,26},{10... | collective-permute-start | bytes 442376 | tf_op jit(solution)/shard_map/ppermute | solution.py:336
  38.9 6.6 %collective-permute-start.8 = (bf16[2,96,384]{2,1,0:T(8,128)(2,1)S(1)}, bf16[2,96,384]{2,1,0:T(8,128)(2,1)S(1)}, u32[]{:S(2)}, u32[]{:S(2)}) collective-permute-start(bf16[2,96,384]{2,1,0:T(8,128)(2,1)S(1)} %get-tuple-element.43.refs_0_), channel_id=1, source_target_pairs={{0,8},{8,0},{16,24},{24,16},{1,9},{9,1},{17,25},{25,17},{2,10},{10... | collective-permute-start | bytes 442376 | tf_op jit(solution)/shard_map/ppermute | solution.py:336
  40.4 7.9 %collective-permute-start.22 = (bf16[2,96,384]{2,1,0:T(8,128)(2,1)S(1)}, bf16[2,96,384]{2,1,0:T(8,128)(2,1)S(1)}, u32[]{:S(2)}, u32[]{:S(2)}) collective-permute-start(bf16[2,96,384]{2,1,0:T(8,128)(2,1)S(1)} %get-tuple-element.56.refs_1_), channel_id=1, source_target_pairs={{0,1},{1,0},{2,3},{3,2},{4,5},{5,4},{6,7},{7,6},{8,9},{9,8},{10,11... | collective-permute-start | bytes 442376 | tf_op jit(solution)/shard_map/ppermute | solution.py:333
  42.2 8.4 %collective-permute-start.19 = (bf16[2,96,384]{2,1,0:T(8,128)(2,1)S(1)}, bf16[2,96,384]{2,1,0:T(8,128)(2,1)S(1)}, u32[]{:S(2)}, u32[]{:S(2)}) collective-permute-start(bf16[2,96,384]{2,1,0:T(8,128)(2,1)S(1)} %collective-permute-done.16.refs_3_), channel_id=1, source_target_pairs={{0,1},{1,0},{2,3},{3,2},{4,5},{5,4},{6,7},{7,6},{8,9},{9,8},{10,11... | collective-permute-start | bytes 442376 | tf_op jit(solution)/shard_map/ppermute | solution.py:333
  42.3 8.3 %collective-permute-start.20 = (bf16[2,96,384]{2,1,0:T(8,128)(2,1)S(1)}, bf16[2,96,384]{2,1,0:T(8,128)(2,1)S(1)}, u32[]{:S(2)}, u32[]{:S(2)}) collective-permute-start(bf16[2,96,384]{2,1,0:T(8,128)(2,1)S(1)} %collective-permute-done.17.refs_4_), channel_id=1, source_target_pairs={{0,1},{1,0},{2,3},{3,2},{4,5},{5,4},{6,7},{7,6},{8,9},{9,8},{10,11... | collective-permute-start | bytes 442376 | tf_op jit(solution)/shard_map/ppermute | solution.py:333
  44.4 6.2 %collective-permute-start.21 = (bf16[2,96,384]{2,1,0:T(8,128)(2,1)S(1)}, bf16[2,96,384]{2,1,0:T(8,128)(2,1)S(1)}, u32[]{:S(2)}, u32[]{:S(2)}) collective-permute-start(bf16[2,96,384]{2,1,0:T(8,128)(2,1)S(1)} %collective-permute-done.18.refs_5_), channel_id=1, source_target_pairs={{0,1},{1,0},{2,3},{3,2},{4,5},{5,4},{6,7},{7,6},{8,9},{9,8},{10,11... | collective-permute-start | bytes 442376 | tf_op jit(solution)/shard_map/ppermute | solution.py:333
  (1 other events, 21.5 us)
where the time goes:
time: 54.7 us; the launch traced here: 54.5 us
  starting transfers between devices  23.8 us (44%)
  Pallas kernels  18.4 us (34%)
  waiting for transfers between devices  12 us (22%)
    ppermute x5, starting transfers between devices, along(): return lax.ppermute(x, 'snk', [(i, i ^ d) for i in range(nsnk)])  9.77 us
    ppermute x9, starting transfers between devices, cross(): return lax.ppermute(x, 'src', [(i, i ^ k) for i in range(nsrc)])  9.56 us
    ppermute x9, waiting for transfers between devices, cross(): return lax.ppermute(x, 'src', [(i, i ^ k) for i in range(nsrc)])  8.56 us
    pallas_call x2, Pallas kernels, finish(): pl.pallas_call(functools.partial(block_kernel, which, chained), out_shape...  5.99 us
    pallas_call x1, Pallas kernels, fast(): pl.pallas_call(functools.partial(own_kernel, nsrc, slabs, lz, sent), out_...  4.03 us
    ppermute x3, starting transfers between devices, far(): return lax.ppermute(x, ('src', 'slab'), pairs)  3.47 us
    ppermute x5, waiting for transfers between devices, along(): return lax.ppermute(x, 'snk', [(i, i ^ d) for i in range(nsnk)])  3.4 us
    pallas_call x1, Pallas kernels, fast(): pl.pallas_call(functools.partial(same_kernel, sent), out_shape=[shape((ro...  2.88 us
  transfers between devices with their start and end apart: 23, of which 8 were waited for; matrix products, arithmetic and copies ran while one was open for 0% of the time, Pallas kernels for 22%

commit v1 on v0

--- a/solution.py
+++ b/solution.py
@@ -16,7 +16,6 @@
 F32 = jnp.float32
 BF16 = jnp.bfloat16
 VMEM = pl.BlockSpec(memory_space=pltpu.VMEM)
-SMEM = pl.BlockSpec(memory_space=pltpu.SMEM)
 
 
 def angles(momenta, xs, ys, zs, lz):
@@ -230,7 +229,7 @@
     for k in range(nsrc):
         for s in range(outs[k].shape[0]):
             if k == 0:
-                want = jnp.full((TAIL, 128), times_ref[s].astype(F32), F32)
+                want = jnp.broadcast_to(times_ref[:, s : s + 1].astype(F32), (TAIL, 128))
             else:
                 want = sent[k - 1][rows + s * TAIL : rows + (s + 1) * TAIL, :128].astype(F32)
             mask = []
@@ -293,14 +292,14 @@
             for at, x in ((0, lower), (rows, upper)):
                 rhs[part, at : at + rows, :] = x
                 rhs[part, nev + at : nev + at + rows, :] = (-turned(x.astype(F32), nev)).astype(BF16)
-            out = lax.dot_general(
-                half[j][s].reshape(tdev * nq * rows, width),
-                rhs[part],
-                (((1,), (1,)), ((), ())),
-                preferred_element_type=F32,
-            )
-            buf[slot] = out.reshape(tdev, nq, rows, width)
             for t in range(tdev):
+                out = lax.dot_general(
+                    half[j][s, t * nq : (t + 1) * nq].reshape(nq * rows, width),
+                    rhs[part],
+                    (((1,), (1,)), ((), ())),
+                    preferred_element_type=F32,
+                )
+                buf[slot, t] = out.reshape(nq, rows, width)
                 copies.append(
                     pltpu.make_async_copy(
                         buf.at[slot, t], out_hbm.at[src ^ k, t, s], sem.at[slot, t]
@@ -433,10 +432,10 @@
         return pl.pallas_call(
             functools.partial(pick_kernel, nsrc, [labels[i] for i in which], bool(before)),
             out_shape=[shape((sdev, rows, width))] * nsrc,
-            in_specs=[SMEM] + [VMEM] * (nsrc - 1 + len(which) + len(before)),
+            in_specs=[VMEM] * (nsrc + len(which) + len(before)),
             out_specs=[VMEM] * nsrc,
             compiler_params=params(8),
-        )(source_times, *got, *(seen[i] for i in which), *before)
+        )(source_times.reshape(1, sdev), *got, *(seen[i] for i in which), *before)
 
     late = len(labels) - 1
     picked = pick(list(range(late)), [])

time: 54.7 us -> 53.7 us (0.982)
  Pallas kernels: 18.4 us -> 16.9 us
  waiting for transfers between devices: 12 us -> 12.9 us
    pallas_call x2, Pallas kernels: 1.61 us -> 0.53 us  [pick(): pl.pallas_call(functools.partial(pick_kernel, nsrc, [labels[i] for i in w...]
  transfers between devices with their start and end apart: 23 -> 23, of which waited for: 8 -> 8; matrix products, arithmetic and copies ran while one was open for 0% -> 0% of each run, Pallas kernels for 22% -> 20%
where the time goes in v1:
time: 53.7 us; the launch traced here: 53.5 us
  starting transfers between devices  23.4 us (44%)
  Pallas kernels  16.9 us (31%)
  waiting for transfers between devices  12.9 us (24%)
    ppermute x5, starting transfers between devices, along(): return lax.ppermute(x, 'snk', [(i, i ^ d) for i in range(nsnk)])  9.77 us
    ppermute x9, starting transfers between devices, cross(): return lax.ppermute(x, 'src', [(i, i ^ k) for i in range(nsrc)])  9.56 us
    ppermute x9, waiting for transfers between devices, cross(): return lax.ppermute(x, 'src', [(i, i ^ k) for i in range(nsrc)])  8.96 us
    pallas_call x2, Pallas kernels, finish(): pl.pallas_call(functools.partial(block_kernel, which, chained), out_shape...  5.58 us
    pallas_call x1, Pallas kernels, fast(): pl.pallas_call(functools.partial(own_kernel, nsrc, slabs, lz, sent), out_...  4.03 us
    ppermute x5, waiting for transfers between devices, along(): return lax.ppermute(x, 'snk', [(i, i ^ d) for i in range(nsnk)])  3.95 us
    ppermute x3, starting transfers between devices, far(): return lax.ppermute(x, ('src', 'slab'), pairs)  3.47 us
    pallas_call x1, Pallas kernels, fast(): pl.pallas_call(functools.partial(same_kernel, sent), out_shape=[shape((ro...  2.88 us
  transfers between devices with their start and end apart: 23, of which 8 were waited for; matrix products, arithmetic and copies ran while one was open for 0% of the time, Pallas kernels for 20%

profile of v1, /device:TPU:0, one launch (start us, length us, event | category | flops | bytes accessed | tf_op | source)
XLA Modules:
  0.0 53.5 jit_solution(15562362301374706336)
XLA Ops:
  0.5 4.0 %gram_own.1 = (f32[4,192,384]{2,1,0:T(8,128)S(1)}, f32[6,4,32,128]{3,2,1,0:T(8,128)S(1)}) custom-call(s32[4,3]{1,0:T(4,128)} %mom_hbm.1, bf16[2,1024,384]{2,1,0:T(8,128)(2,1)} %eig_hbm.1), custom_call_target="tpu_custom_call" | custom-call | flops 1207959552 | bytes 786432 | tf_op jit(solution)/shard_map/gram_own/pallas_call | solution.py:363
  4.5 2.9 %gram_same.1 = (bf16[128,384]{1,0:T(8,128)(2,1)S(1)}, bf16[128,384]{1,0:T(8,128)(2,1)S(1)}, bf16[128,384]{1,0:T(8,128)(2,1)S(1)}, f32[96,384]{1,0:T(8,128)S(1)},...) custom-call(s32[1,2]{1,0:T(1,128)} %bitcast.1, bf16[2,1024,384]{2,1,0:T(8,128)(2,1)S(1)} %collective-permute-done.eig_ref, ...), custom_call_target="tpu_custom_call" | custom-call | flops 603979776 | bytes 786432 | tf_op jit(solution)/shard_map/gram_same/pallas_call | solution.py:373
  7.4 2.5 %collective-permute-start.5 = (bf16[128,384]{1,0:T(8,128)(2,1)S(1)}, bf16[128,384]{1,0:T(8,128)(2,1)S(1)}, u32[]{:S(2)}, u32[]{:S(2)}) collective-permute-start(bf16[128,384]{1,0:T(8,128)(2,1)S(1)} %get-tuple-element.40), channel_id=1, source_target_pairs={{0,8},{8,0},{16,24},{24,16},{1,9},{9,1},{17,25},{25,17},{2,10},{10... | collective-permute-start | bytes 294920 | tf_op jit(solution)/shard_map/ppermute | solution.py:335
  10.0 1.5 %collective-permute-start.6 = (bf16[128,384]{1,0:T(8,128)(2,1)S(1)}, bf16[128,384]{1,0:T(8,128)(2,1)S(1)}, u32[]{:S(2)}, u32[]{:S(2)}) collective-permute-start(bf16[128,384]{1,0:T(8,128)(2,1)S(1)} %get-tuple-element.41), channel_id=1, source_target_pairs={{0,16},{8,24},{16,0},{24,8},{1,17},{9,25},{17,1},{25,9},{2,18},{10... | collective-permute-start | bytes 294920 | tf_op jit(solution)/shard_map/ppermute | solution.py:335
  11.5 1.1 %gram_cross.1 = (bf16[96,384]{1,0:T(8,128)(2,1)S(1)}, bf16[96,384]{1,0:T(8,128)(2,1)S(1)}, bf16[96,384]{1,0:T(8,128)(2,1)S(1)}, f32[96,384]{1,0:T(8,128)S(1)}) custom-call(bf16[1024,1536]{1,0:T(8,128)(2,1)S(1)} %get-tuple-element.33.wide, bf16[192,1024]{1,0:T(8,128)(2,1)S(1)} %get-tuple-element.34.rest, f32[4,192,384]{2,1,0:T(8,128)S(1)} %get-tuple-element.32.acc_ref), custom_call_target="tpu_custom_call" | custom-call | flops 603979776 | bytes 786432 | tf_op jit(solution)/shard_map/gram_cross/pallas_call | solution.py:391
  12.9 1.6 %collective-permute-start.2 = (bf16[96,384]{1,0:T(8,128)(2,1)S(1)}, bf16[96,384]{1,0:T(8,128)(2,1)S(1)}, u32[]{:S(2)}, u32[]{:S(2)}) collective-permute-start(bf16[96,384]{1,0:T(8,128)(2,1)S(1)} %get-tuple-element.36), channel_id=1, source_target_pairs={{0,9},{1,8},{8,1},{9,0},{16,25},{17,24},{24,17},{25,16},{2,11},{3,... | collective-permute-start | bytes 221192 | tf_op jit(solution)/shard_map/ppermute | solution.py:339
  14.4 1.5 %collective-permute-start.3 = (bf16[96,384]{1,0:T(8,128)(2,1)S(1)}, bf16[96,384]{1,0:T(8,128)(2,1)S(1)}, u32[]{:S(2)}, u32[]{:S(2)}) collective-permute-start(bf16[96,384]{1,0:T(8,128)(2,1)S(1)} %get-tuple-element.37), channel_id=1, source_target_pairs={{0,17},{1,16},{8,25},{9,24},{16,1},{17,0},{24,9},{25,8},{2,19},{3,... | collective-permute-start | bytes 221192 | tf_op jit(solution)/shard_map/ppermute | solution.py:339
  16.4 2.9 %collective-permute-done.7.refs_2_ = bf16[128,384]{1,0:T(8,128)(2,1)S(1)} collective-permute-done((bf16[128,384]{1,0:T(8,128)(2,1)S(1)}, bf16[128,384]{1,0:T(8,128)(2,1)S(1)}, u32[]{:S(2)}, u32[]{:S(2)}) %collective-permute-start.7) | collective-permute-done | bytes 98336 | tf_op jit(solution)/shard_map/ppermute | solution.py:335
  19.3 2.7 %collective-permute-start.13 = (bf16[96,384]{1,0:T(8,128)(2,1)S(1)}, bf16[96,384]{1,0:T(8,128)(2,1)S(1)}, u32[]{:S(2)}, u32[]{:S(2)}) collective-permute-start(bf16[96,384]{1,0:T(8,128)(2,1)S(1)} %sum_same.1.refs_3_), channel_id=1, source_target_pairs={{0,4},{2,6},{4,0},{6,2},{1,5},{3,7},{5,1},{7,3},{8,12},{10,14},{12... | collective-permute-start | bytes 221192 | tf_op jit(solution)/shard_map/ppermute | solution.py:342
  22.1 1.6 %collective-permute-start.14 = (bf16[2,96,384]{2,1,0:T(8,128)(2,1)S(1)}, bf16[2,96,384]{2,1,0:T(8,128)(2,1)S(1)}, u32[]{:S(2)}, u32[]{:S(2)}) collective-permute-start(bf16[2,96,384]{2,1,0:T(8,128)(2,1)S(1)} %get-tuple-element.43.refs_0_), channel_id=1, source_target_pairs={{0,2},{2,0},{4,6},{6,4},{1,3},{3,1},{5,7},{7,5},{8,10},{10,8},{12,... | collective-permute-start | bytes 442376 | tf_op jit(solution)/shard_map/ppermute | solution.py:342
  23.7 2.0 %collective-permute-start.11 = (bf16[96,384]{1,0:T(8,128)(2,1)S(1)}, bf16[96,384]{1,0:T(8,128)(2,1)S(1)}, u32[]{:S(2)}, u32[]{:S(2)}) collective-permute-start(bf16[96,384]{1,0:T(8,128)(2,1)S(1)} %get-tuple-element.47.refs_4_), channel_id=1, source_target_pairs={{0,4},{2,6},{4,0},{6,2},{1,5},{3,7},{5,1},{7,3},{8,12},{10,14},{12... | collective-permute-start | bytes 221192 | tf_op jit(solution)/shard_map/ppermute | solution.py:342
  26.7 2.7 %collective-permute-done.11.refs_6_ = bf16[96,384]{1,0:T(8,128)(2,1)S(1)} collective-permute-done((bf16[96,384]{1,0:T(8,128)(2,1)S(1)}, bf16[96,384]{1,0:T(8,128)(2,1)S(1)}, u32[]{:S(2)}, u32[]{:S(2)}) %collective-permute-start.11) | collective-permute-done | bytes 73760 | tf_op jit(solution)/shard_map/ppermute | solution.py:342
  29.4 3.0 %collective-permute-start.12 = (bf16[96,384]{1,0:T(8,128)(2,1)S(1)}, bf16[96,384]{1,0:T(8,128)(2,1)S(1)}, u32[]{:S(2)}, u32[]{:S(2)}) collective-permute-start(bf16[96,384]{1,0:T(8,128)(2,1)S(1)} %collective-permute-done.11.refs_6_), channel_id=1, source_target_pairs={{0,2},{2,0},{4,6},{6,4},{1,3},{3,1},{5,7},{7,5},{8,10},{10,8},{12,... | collective-permute-start | bytes 221192 | tf_op jit(solution)/shard_map/ppermute | solution.py:342
  33.5 1.3 %collective-permute-done.12.refs_3_ = bf16[96,384]{1,0:T(8,128)(2,1)S(1)} collective-permute-done((bf16[96,384]{1,0:T(8,128)(2,1)S(1)}, bf16[96,384]{1,0:T(8,128)(2,1)S(1)}, u32[]{:S(2)}, u32[]{:S(2)}) %collective-permute-start.12) | collective-permute-done | bytes 73760 | tf_op jit(solution)/shard_map/ppermute | solution.py:342
  35.5 0.6 %collective-permute-start.17 = (bf16[2,96,384]{2,1,0:T(8,128)(2,1)S(1)}, bf16[2,96,384]{2,1,0:T(8,128)(2,1)S(1)}, u32[]{:S(2)}, u32[]{:S(2)}) collective-permute-start(bf16[2,96,384]{2,1,0:T(8,128)(2,1)S(1)} %get-tuple-element.53), channel_id=1, source_target_pairs={{0,16},{8,24},{16,0},{24,8},{1,17},{9,25},{17,1},{25,9},{2,18},{10... | collective-permute-start | bytes 442376 | tf_op jit(solution)/shard_map/ppermute | solution.py:335
  36.1 2.3 %collective-permute-start.18 = (bf16[2,96,384]{2,1,0:T(8,128)(2,1)S(1)}, bf16[2,96,384]{2,1,0:T(8,128)(2,1)S(1)}, u32[]{:S(2)}, u32[]{:S(2)}) collective-permute-start(bf16[2,96,384]{2,1,0:T(8,128)(2,1)S(1)} %get-tuple-element.54), channel_id=1, source_target_pairs={{0,24},{8,16},{16,8},{24,0},{1,25},{9,17},{17,9},{25,1},{2,26},{10... | collective-permute-start | bytes 442376 | tf_op jit(solution)/shard_map/ppermute | solution.py:335
  38.9 1.5 %collective-permute-done.9.refs_2_ = bf16[2,96,384]{2,1,0:T(8,128)(2,1)S(1)} collective-permute-done((bf16[2,96,384]{2,1,0:T(8,128)(2,1)S(1)}, bf16[2,96,384]{2,1,0:T(8,128)(2,1)S(1)}, u32[]{:S(2)}, u32[]{:S(2)}) %collective-permute-start.9) | collective-permute-done | bytes 147488 | tf_op jit(solution)/shard_map/ppermute | solution.py:335
  40.5 1.2 %collective-permute-done.16.refs_3_ = bf16[2,96,384]{2,1,0:T(8,128)(2,1)S(1)} collective-permute-done((bf16[2,96,384]{2,1,0:T(8,128)(2,1)S(1)}, bf16[2,96,384]{2,1,0:T(8,128)(2,1)S(1)}, u32[]{:S(2)}, u32[]{:S(2)}) %collective-permute-start.16) | collective-permute-done | bytes 147488 | tf_op jit(solution)/shard_map/ppermute | solution.py:335
  41.6 0.8 %collective-permute-done.17.refs_4_ = bf16[2,96,384]{2,1,0:T(8,128)(2,1)S(1)} collective-permute-done((bf16[2,96,384]{2,1,0:T(8,128)(2,1)S(1)}, bf16[2,96,384]{2,1,0:T(8,128)(2,1)S(1)}, u32[]{:S(2)}, u32[]{:S(2)}) %collective-permute-start.17) | collective-permute-done | bytes 147488 | tf_op jit(solution)/shard_map/ppermute | solution.py:335
  42.4 1.2 %collective-permute-done.18.refs_5_ = bf16[2,96,384]{2,1,0:T(8,128)(2,1)S(1)} collective-permute-done((bf16[2,96,384]{2,1,0:T(8,128)(2,1)S(1)}, bf16[2,96,384]{2,1,0:T(8,128)(2,1)S(1)}, u32[]{:S(2)}, u32[]{:S(2)}) %collective-permute-start.18) | collective-permute-done | bytes 147488 | tf_op jit(solution)/shard_map/ppermute | solution.py:335
  43.6 1.4 %collective-permute-done.8.refs_1_ = bf16[2,96,384]{2,1,0:T(8,128)(2,1)S(1)} collective-permute-done((bf16[2,96,384]{2,1,0:T(8,128)(2,1)S(1)}, bf16[2,96,384]{2,1,0:T(8,128)(2,1)S(1)}, u32[]{:S(2)}, u32[]{:S(2)}) %collective-permute-start.8) | collective-permute-done | bytes 147488 | tf_op jit(solution)/shard_map/ppermute | solution.py:335
  45.0 2.7 %shard_map.46 = (bf16[2,8,96,384]{3,2,1,0:T(8,128)(2,1)S(1)}, bf16[2,8,96,384]{3,2,1,0:T(8,128)(2,1)S(1)}, bf16[2,8,96,384]{3,2,1,0:T(8,128)(2,1)S(1)}, bf16[2,8,96,384]{3,2,1,0:T(8,128)(2,1)S(1)}) custom-call(bf16[2,96,384]{2,1,0:T(8,128)(2,1)S(1)} %get-tuple-element.43.refs_0_, bf16[2,96,384]{2,1,0:T(8,128)(2,1)S(1)} %collective-permute-done.8.refs_1_, ...), custom_call_target="tpu_custom_call" | custom-call | flops 1811939328 | bytes 2359296 | tf_op jit(solution)/shard_map/pallas_call | solution.py:448
  47.7 2.1 %shard_map.49.refs_9_ = f32[4,2,2,4,96,384]{5,4,3,2,1,0:T(8,128)} custom-call(bf16[2,8,96,384]{3,2,1,0:T(8,128)(2,1)S(1)} %get-tuple-element.55.refs_0_, bf16[2,96,384]{2,1,0:T(8,128)(2,1)S(1)} %get-tuple-element.56.refs_1_, bf16[2,96,384]{2,1,0:T(8,128)(2,1)S(1)} %collective-permute-done.22.refs_2_), custom_call_target="tpu_custom_call" | custom-call | flops 452984832 | bytes 2359296 | tf_op jit(solution)/shard_map/pallas_call | solution.py:470
  49.9 3.5 %shard_map.50 = f32[4,2,2,4,96,384]{5,4,3,2,1,0:T(8,128)} custom-call(bf16[2,8,96,384]{3,2,1,0:T(8,128)(2,1)S(1)} %get-tuple-element.44.refs_0_, bf16[2,8,96,384]{3,2,1,0:T(8,128)(2,1)S(1)} %get-tuple-element.45.refs_1_, bf16[2,8,96,384]{3,2,1,0:T(8,128)(2,1)S(1)} %get-tuple-element.46.refs_2_, ...), custom_call_target="tpu_custom_call", output_to_operand_aliasing={{}: (9, {})} | custom-call | flops 1358954496 | bytes 7077888 | tf_op jit(solution)/shard_map/pallas_call | solution.py:470
  (36 shorter events, 4.7 us)
Async XLA Ops:
  0.0 4.5 %collective-permute-start = (bf16[2,1024,384]{2,1,0:T(8,128)(2,1)}, bf16[2,1024,384]{2,1,0:T(8,128)(2,1)S(1)}, u32[]{:S(2)}, u32[]{:S(2)}) collective-permute-start(bf16[2,1024,384]{2,1,0:T(8,128)(2,1)} %eig_hbm.1), channel_id=1, source_target_pairs={{0,1},{1,0},{2,3},{3,2},{4,5},{5,4},{6,7},{7,6},{8,9},{9,8},{10,11... | collective-permute-start | bytes 4718600 | tf_op jit(solution)/shard_map/ppermute | solution.py:332
  7.4 7.0 %collective-permute-start.5 = (bf16[128,384]{1,0:T(8,128)(2,1)S(1)}, bf16[128,384]{1,0:T(8,128)(2,1)S(1)}, u32[]{:S(2)}, u32[]{:S(2)}) collective-permute-start(bf16[128,384]{1,0:T(8,128)(2,1)S(1)} %get-tuple-element.40), channel_id=1, source_target_pairs={{0,8},{8,0},{16,24},{24,16},{1,9},{9,1},{17,25},{25,17},{2,10},{10... | collective-permute-start | bytes 294920 | tf_op jit(solution)/shard_map/ppermute | solution.py:335
  10.0 6.0 %collective-permute-start.6 = (bf16[128,384]{1,0:T(8,128)(2,1)S(1)}, bf16[128,384]{1,0:T(8,128)(2,1)S(1)}, u32[]{:S(2)}, u32[]{:S(2)}) collective-permute-start(bf16[128,384]{1,0:T(8,128)(2,1)S(1)} %get-tuple-element.41), channel_id=1, source_target_pairs={{0,16},{8,24},{16,0},{24,8},{1,17},{9,25},{17,1},{25,9},{2,18},{10... | collective-permute-start | bytes 294920 | tf_op jit(solution)/shard_map/ppermute | solution.py:335
  12.5 32.5 %copy-start.1 = (bf16[2,2,4,192,384]{4,3,2,1,0:T(8,128)(2,1)S(1)}, bf16[2,2,4,192,384]{4,3,2,1,0:T(8,128)(2,1)}, u32[]{:S(2)}) copy-start(bf16[2,2,4,192,384]{4,3,2,1,0:T(8,128)(2,1)} %refs_4_.1) | copy-start | bytes 7077892
  12.6 9.4 %collective-permute-start.1 = (f32[96,384]{1,0:T(8,128)S(1)}, f32[96,384]{1,0:T(8,128)S(1)}, u32[]{:S(2)}, u32[]{:S(2)}) collective-permute-start(f32[96,384]{1,0:T(8,128)S(1)} %get-tuple-element.35), channel_id=1, source_target_pairs={{0,1},{1,0},{2,3},{3,2},{4,5},{5,4},{6,7},{7,6},{8,9},{9,8},{10,11... | collective-permute-start | bytes 442376 | tf_op jit(solution)/shard_map/ppermute | solution.py:332
  12.6 6.6 %collective-permute-start.7 = (bf16[128,384]{1,0:T(8,128)(2,1)S(1)}, bf16[128,384]{1,0:T(8,128)(2,1)S(1)}, u32[]{:S(2)}, u32[]{:S(2)}) collective-permute-start(bf16[128,384]{1,0:T(8,128)(2,1)S(1)} %get-tuple-element.42), channel_id=1, source_target_pairs={{0,24},{8,16},{16,8},{24,0},{1,25},{9,17},{17,9},{25,1},{2,26},{10... | collective-permute-start | bytes 294920 | tf_op jit(solution)/shard_map/ppermute | solution.py:335
  12.9 9.1 %collective-permute-start.2 = (bf16[96,384]{1,0:T(8,128)(2,1)S(1)}, bf16[96,384]{1,0:T(8,128)(2,1)S(1)}, u32[]{:S(2)}, u32[]{:S(2)}) collective-permute-start(bf16[96,384]{1,0:T(8,128)(2,1)S(1)} %get-tuple-element.36), channel_id=1, source_target_pairs={{0,9},{1,8},{8,1},{9,0},{16,25},{17,24},{24,17},{25,16},{2,11},{3,... | collective-permute-start | bytes 221192 | tf_op jit(solution)/shard_map/ppermute | solution.py:339
  14.4 7.5 %collective-permute-start.3 = (bf16[96,384]{1,0:T(8,128)(2,1)S(1)}, bf16[96,384]{1,0:T(8,128)(2,1)S(1)}, u32[]{:S(2)}, u32[]{:S(2)}) collective-permute-start(bf16[96,384]{1,0:T(8,128)(2,1)S(1)} %get-tuple-element.37), channel_id=1, source_target_pairs={{0,17},{1,16},{8,25},{9,24},{16,1},{17,0},{24,9},{25,8},{2,19},{3,... | collective-permute-start | bytes 221192 | tf_op jit(solution)/shard_map/ppermute | solution.py:339
  15.9 6.1 %collective-permute-start.4 = (bf16[96,384]{1,0:T(8,128)(2,1)S(1)}, bf16[96,384]{1,0:T(8,128)(2,1)S(1)}, u32[]{:S(2)}, u32[]{:S(2)}) collective-permute-start(bf16[96,384]{1,0:T(8,128)(2,1)S(1)} %get-tuple-element.38), channel_id=1, source_target_pairs={{0,25},{1,24},{8,17},{9,16},{16,9},{17,8},{24,1},{25,0},{2,27},{3,... | collective-permute-start | bytes 221192 | tf_op jit(solution)/shard_map/ppermute | solution.py:339
  19.3 6.9 %collective-permute-start.13 = (bf16[96,384]{1,0:T(8,128)(2,1)S(1)}, bf16[96,384]{1,0:T(8,128)(2,1)S(1)}, u32[]{:S(2)}, u32[]{:S(2)}) collective-permute-start(bf16[96,384]{1,0:T(8,128)(2,1)S(1)} %sum_same.1.refs_3_), channel_id=1, source_target_pairs={{0,4},{2,6},{4,0},{6,2},{1,5},{3,7},{5,1},{7,3},{8,12},{10,14},{12... | collective-permute-start | bytes 221192 | tf_op jit(solution)/shard_map/ppermute | solution.py:342
  22.1 11.0 %collective-permute-start.14 = (bf16[2,96,384]{2,1,0:T(8,128)(2,1)S(1)}, bf16[2,96,384]{2,1,0:T(8,128)(2,1)S(1)}, u32[]{:S(2)}, u32[]{:S(2)}) collective-permute-start(bf16[2,96,384]{2,1,0:T(8,128)(2,1)S(1)} %get-tuple-element.43.refs_0_), channel_id=1, source_target_pairs={{0,2},{2,0},{4,6},{6,4},{1,3},{3,1},{5,7},{7,5},{8,10},{10,8},{12,... | collective-permute-start | bytes 442376 | tf_op jit(solution)/shard_map/ppermute | solution.py:342
  23.7 5.7 %collective-permute-start.11 = (bf16[96,384]{1,0:T(8,128)(2,1)S(1)}, bf16[96,384]{1,0:T(8,128)(2,1)S(1)}, u32[]{:S(2)}, u32[]{:S(2)}) collective-permute-start(bf16[96,384]{1,0:T(8,128)(2,1)S(1)} %get-tuple-element.47.refs_4_), channel_id=1, source_target_pairs={{0,4},{2,6},{4,0},{6,2},{1,5},{3,7},{5,1},{7,3},{8,12},{10,14},{12... | collective-permute-start | bytes 221192 | tf_op jit(solution)/shard_map/ppermute | solution.py:342
  25.7 12.7 %collective-permute-start.10 = (bf16[2,96,384]{2,1,0:T(8,128)(2,1)S(1)}, bf16[2,96,384]{2,1,0:T(8,128)(2,1)S(1)}, u32[]{:S(2)}, u32[]{:S(2)}) collective-permute-start(bf16[2,96,384]{2,1,0:T(8,128)(2,1)S(1)} %get-tuple-element.43.refs_0_), channel_id=1, source_target_pairs={{0,24},{8,16},{16,8},{24,0},{1,25},{9,17},{17,9},{25,1},{2,26},{10... | collective-permute-start | bytes 442376 | tf_op jit(solution)/shard_map/ppermute | solution.py:335
  26.3 6.8 %collective-permute-start.15 = (bf16[96,384]{1,0:T(8,128)(2,1)S(1)}, bf16[96,384]{1,0:T(8,128)(2,1)S(1)}, u32[]{:S(2)}, u32[]{:S(2)}) collective-permute-start(bf16[96,384]{1,0:T(8,128)(2,1)S(1)} %collective-permute-done.13.refs_5_), channel_id=1, source_target_pairs={{0,2},{2,0},{4,6},{6,4},{1,3},{3,1},{5,7},{7,5},{8,10},{10,8},{12,... | collective-permute-start | bytes 221192 | tf_op jit(solution)/shard_map/ppermute | solution.py:342
  29.4 5.4 %collective-permute-start.12 = (bf16[96,384]{1,0:T(8,128)(2,1)S(1)}, bf16[96,384]{1,0:T(8,128)(2,1)S(1)}, u32[]{:S(2)}, u32[]{:S(2)}) collective-permute-start(bf16[96,384]{1,0:T(8,128)(2,1)S(1)} %collective-permute-done.11.refs_6_), channel_id=1, source_target_pairs={{0,2},{2,0},{4,6},{6,4},{1,3},{3,1},{5,7},{7,5},{8,10},{10,8},{12,... | collective-permute-start | bytes 221192 | tf_op jit(solution)/shard_map/ppermute | solution.py:342
  32.4 8.1 %collective-permute-start.9 = (bf16[2,96,384]{2,1,0:T(8,128)(2,1)S(1)}, bf16[2,96,384]{2,1,0:T(8,128)(2,1)S(1)}, u32[]{:S(2)}, u32[]{:S(2)}) collective-permute-start(bf16[2,96,384]{2,1,0:T(8,128)(2,1)S(1)} %get-tuple-element.43.refs_0_), channel_id=1, source_target_pairs={{0,16},{8,24},{16,0},{24,8},{1,17},{9,25},{17,1},{25,9},{2,18},{10... | collective-permute-start | bytes 442376 | tf_op jit(solution)/shard_map/ppermute | solution.py:335
  34.8 6.8 %collective-permute-start.16 = (bf16[2,96,384]{2,1,0:T(8,128)(2,1)S(1)}, bf16[2,96,384]{2,1,0:T(8,128)(2,1)S(1)}, u32[]{:S(2)}, u32[]{:S(2)}) collective-permute-start(bf16[2,96,384]{2,1,0:T(8,128)(2,1)S(1)} %get-tuple-element.52), channel_id=1, source_target_pairs={{0,8},{8,0},{16,24},{24,16},{1,9},{9,1},{17,25},{25,17},{2,10},{10... | collective-permute-start | bytes 442376 | tf_op jit(solution)/shard_map/ppermute | solution.py:335
  35.5 7.0 %collective-permute-start.17 = (bf16[2,96,384]{2,1,0:T(8,128)(2,1)S(1)}, bf16[2,96,384]{2,1,0:T(8,128)(2,1)S(1)}, u32[]{:S(2)}, u32[]{:S(2)}) collective-permute-start(bf16[2,96,384]{2,1,0:T(8,128)(2,1)S(1)} %get-tuple-element.53), channel_id=1, source_target_pairs={{0,16},{8,24},{16,0},{24,8},{1,17},{9,25},{17,1},{25,9},{2,18},{10... | collective-permute-start | bytes 442376 | tf_op jit(solution)/shard_map/ppermute | solution.py:335
  36.1 7.6 %collective-permute-start.18 = (bf16[2,96,384]{2,1,0:T(8,128)(2,1)S(1)}, bf16[2,96,384]{2,1,0:T(8,128)(2,1)S(1)}, u32[]{:S(2)}, u32[]{:S(2)}) collective-permute-start(bf16[2,96,384]{2,1,0:T(8,128)(2,1)S(1)} %get-tuple-element.54), channel_id=1, source_target_pairs={{0,24},{8,16},{16,8},{24,0},{1,25},{9,17},{17,9},{25,1},{2,26},{10... | collective-permute-start | bytes 442376 | tf_op jit(solution)/shard_map/ppermute | solution.py:335
  38.4 6.6 %collective-permute-start.8 = (bf16[2,96,384]{2,1,0:T(8,128)(2,1)S(1)}, bf16[2,96,384]{2,1,0:T(8,128)(2,1)S(1)}, u32[]{:S(2)}, u32[]{:S(2)}) collective-permute-start(bf16[2,96,384]{2,1,0:T(8,128)(2,1)S(1)} %get-tuple-element.43.refs_0_), channel_id=1, source_target_pairs={{0,8},{8,0},{16,24},{24,16},{1,9},{9,1},{17,25},{25,17},{2,10},{10... | collective-permute-start | bytes 442376 | tf_op jit(solution)/shard_map/ppermute | solution.py:335
  40.5 7.3 %collective-permute-start.22 = (bf16[2,96,384]{2,1,0:T(8,128)(2,1)S(1)}, bf16[2,96,384]{2,1,0:T(8,128)(2,1)S(1)}, u32[]{:S(2)}, u32[]{:S(2)}) collective-permute-start(bf16[2,96,384]{2,1,0:T(8,128)(2,1)S(1)} %get-tuple-element.56.refs_1_), channel_id=1, source_target_pairs={{0,1},{1,0},{2,3},{3,2},{4,5},{5,4},{6,7},{7,6},{8,9},{9,8},{10,11... | collective-permute-start | bytes 442376 | tf_op jit(solution)/shard_map/ppermute | solution.py:332
  41.6 8.2 %collective-permute-start.19 = (bf16[2,96,384]{2,1,0:T(8,128)(2,1)S(1)}, bf16[2,96,384]{2,1,0:T(8,128)(2,1)S(1)}, u32[]{:S(2)}, u32[]{:S(2)}) collective-permute-start(bf16[2,96,384]{2,1,0:T(8,128)(2,1)S(1)} %collective-permute-done.16.refs_3_), channel_id=1, source_target_pairs={{0,1},{1,0},{2,3},{3,2},{4,5},{5,4},{6,7},{7,6},{8,9},{9,8},{10,11... | collective-permute-start | bytes 442376 | tf_op jit(solution)/shard_map/ppermute | solution.py:332
  42.4 7.4 %collective-permute-start.20 = (bf16[2,96,384]{2,1,0:T(8,128)(2,1)S(1)}, bf16[2,96,384]{2,1,0:T(8,128)(2,1)S(1)}, u32[]{:S(2)}, u32[]{:S(2)}) collective-permute-start(bf16[2,96,384]{2,1,0:T(8,128)(2,1)S(1)} %collective-permute-done.17.refs_4_), channel_id=1, source_target_pairs={{0,1},{1,0},{2,3},{3,2},{4,5},{5,4},{6,7},{7,6},{8,9},{9,8},{10,11... | collective-permute-start | bytes 442376 | tf_op jit(solution)/shard_map/ppermute | solution.py:332
  43.6 6.2 %collective-permute-start.21 = (bf16[2,96,384]{2,1,0:T(8,128)(2,1)S(1)}, bf16[2,96,384]{2,1,0:T(8,128)(2,1)S(1)}, u32[]{:S(2)}, u32[]{:S(2)}) collective-permute-start(bf16[2,96,384]{2,1,0:T(8,128)(2,1)S(1)} %collective-permute-done.18.refs_5_), channel_id=1, source_target_pairs={{0,1},{1,0},{2,3},{3,2},{4,5},{5,4},{6,7},{7,6},{8,9},{9,8},{10,11... | collective-permute-start | bytes 442376 | tf_op jit(solution)/shard_map/ppermute | solution.py:332
  (1 other events, 21.5 us)
